TPU v7x, 32 devices: a whole 2x2x4 slice. The times are simulated.
32 devices in a mesh: dp: 8 (over z, x), mlp: 4 (over y, core).
Axes of the slice: x: 2, y: 2, z: 4, core: 2. Of those that a mesh axis runs over, the one named last changes fastest.
Arguments:
- tokens: bfloat16 [32768, 768], P(('dp', 'mlp')), may hold values from -6 to 6
- cotangent: bfloat16 [32768, 768], P(('dp', 'mlp')), may hold values from -6 to 6
- vectors: float32 [14, 768], replicated
- vector_moments: float32 [14, 768], replicated, may hold values from 819.2 to 26214.4
- decays: float32 [2], replicated, may hold values from 0.9 to 0.98
- owner: int32 [4, 3], replicated, may hold values from 0 to 7, as said below
- master_slots: float32 [8, 4, 768, 768], P('dp', 'mlp'), as said below
- left_slots: float32 [8, 4, 768, 768], P('dp', 'mlp'), as said below
- right_slots: float32 [8, 4, 768, 768], P('dp', 'mlp'), as said below
- left_roots: float32 [8, 4, 768, 768], P('dp', 'mlp'), as said below
- right_roots: float32 [8, 4, 768, 768], P('dp', 'mlp'), as said below
- grid_height: int32 [128], P(('dp', 'mlp')), may hold values from 8 to 24, as said below
- grid_width: int32 [128], P(('dp', 'mlp')), may hold values from 8 to 24, as said below
- patch_rows: int32 [32768], P(('dp', 'mlp')), may hold values from 0 to 23, as said below
- patch_cols: int32 [32768], P(('dp', 'mlp')), may hold values from 0 to 23, as said below
- segment: int32 [32768], P(('dp', 'mlp')), may hold values from 0 to 3, as said below
Outputs:
- output: bfloat16 [32768, 768], P(('dp', 'mlp'))
- input_grad: float32 [32768, 768], P(('dp', 'mlp'))
- slot_grads: float32 [8, 4, 768, 768], P('dp', 'mlp')
- new_left: float32 [8, 4, 768, 768], P('dp', 'mlp')
- new_right: float32 [8, 4, 768, 768], P('dp', 'mlp')
- new_master: float32 [8, 4, 768, 768], P('dp', 'mlp')
- vector_grads: float32 [14, 768], P(None, 'mlp')
- new_vector_moments: float32 [14, 768], P(None, 'mlp')
- new_vectors: float32 [14, 768], P(None, 'mlp')
Inputs may be any that keep to these rules, and one draw needn't show every extreme that they name: `owner`: the entries of a row differ; block kind 0 of row m is the m-th of the query, key, value and output projections, kind 1 the m-th 768 columns of the up projection, kind 2 the m-th 768 rows of the down projection. `master_slots`: slot (owner[m,k], m) holds block kind k of row m; the other slots are unused. `left_slots`: symmetric and positive definite. `right_slots`: symmetric and positive definite. `left_roots`: symmetric and positive definite. `right_roots`: symmetric and positive definite. `grid_height`: each image is 16 patches along one side; the other sides of one device's images add up to 64. `grid_width`: as grid_height. `patch_rows`: each device's patches hold its images whole, one after another in the order of their numbers, each in raster order. `patch_cols`: as patch_rows. `segment`: never falls within a device's patches.
All inputs are finite; a program needn't handle non-finite values.
Results may differ from a plain program's by a relative error of at most 0.014.
Values may be sent and summed in bfloat16 or wider, within the bound.
A program may use at most 192 MiB of HBM per device.

v0:
```python
import math
import jax
import jax.numpy as jnp
from jax import lax
from jax.sharding import PartitionSpec as P

HEADS = 12
GRID_BASE = 16
NORM_EPSILON = 1e-06
GRAFT_EPSILON = 1e-06
STEP_EPSILON = 1e-08
RATE_MATRIX = 0.04
RATE_VECTOR = 0.02
MASKED_SCORE = -1e30


def layer_norm(values, gain_row, shift_row):
    centred = values - jnp.mean(values, axis=-1, keepdims=True)
    spread = jnp.mean(centred * centred, axis=-1, keepdims=True)
    return centred * lax.rsqrt(spread + NORM_EPSILON) * gain_row + shift_row


def exact_gelu(values):
    return jax.nn.gelu(values, approximate=False)


def rotate_pairs(flat_values, freq_row, rows_pos, cols_pos):
    tokens_here = flat_values.shape[0]
    values = flat_values.reshape(tokens_here, HEADS, -1)
    half_size = values.shape[-1] // 2
    middle = freq_row.shape[0] // 2
    freq_cols = freq_row[:middle].reshape(HEADS, half_size)
    freq_rows = freq_row[middle:].reshape(HEADS, half_size)
    angle_grid = (
        rows_pos[:, None, None] * freq_rows[None] + cols_pos[:, None, None] * freq_cols[None]
    )
    cosine = jnp.cos(angle_grid)
    sine_part = jnp.sin(angle_grid)
    first_half = values[..., :half_size]
    second = values[..., half_size:]
    turned = jnp.concatenate(
        [first_half * cosine - second * sine_part, second * cosine + first_half * sine_part],
        axis=-1,
    )
    return turned.reshape(tokens_here, -1)


def patch_positions(segment_ids, heights_in, widths_in, rows_in, cols_in):
    images_here = heights_in.shape[0]
    matches = segment_ids[:, None] == jnp.arange(images_here, dtype=jnp.int32)[None, :]
    heights = jnp.sum(jnp.where(matches, heights_in[None, :], 0), axis=1).astype(jnp.float32)
    widths = jnp.sum(jnp.where(matches, widths_in[None, :], 0), axis=1).astype(jnp.float32)
    rows_pos = rows_in.astype(jnp.float32) * GRID_BASE / heights
    cols_pos = cols_in.astype(jnp.float32) * GRID_BASE / widths
    return (rows_pos, cols_pos)


def heads_first(flat_values):
    return jnp.swapaxes(flat_values.reshape(flat_values.shape[0], HEADS, -1), 0, 1)


def tokens_first(stacked):
    return jnp.swapaxes(stacked, 0, 1).reshape(stacked.shape[1], -1)


def local(
    tokens,
    cotangent,
    vectors,
    vector_moments,
    decays,
    owner,
    master_slots,
    left_slots,
    right_slots,
    left_roots,
    right_roots,
    grid_height,
    grid_width,
    patch_rows,
    patch_cols,
    segment,
):
    dp_index = lax.axis_index("dp")
    mlp_index = lax.axis_index("mlp")
    groups_mlp = lax.axis_size("mlp")
    model_width = tokens.shape[1]
    rows_here = tokens.shape[0]
    owner_row = jnp.take(owner, mlp_index, axis=0)
    holds_block = owner_row == dp_index
    owned_blocks = jnp.where(holds_block[:, None, None], master_slots[0, 0][None], 0.0)
    blocks = lax.psum(owned_blocks, "dp")
    blocks_low = blocks.astype(jnp.bfloat16)
    up_rows = vectors[8 : 8 + groups_mlp]
    down_bias = vectors[8 + groups_mlp]
    freq_row = vectors[9 + groups_mlp]
    every_block = lax.all_gather(blocks_low[None], "mlp", axis=0, tiled=True)
    attention_weights = every_block[:, 0]
    up_weight = every_block[:, 1]
    down_weight = every_block[:, 2]
    up_bias = up_rows.reshape(-1)
    inputs = tokens.astype(jnp.float32)
    norm_one, norm_one_back = jax.vjp(layer_norm, inputs, vectors[0], vectors[1])
    norm_one_low = norm_one.astype(jnp.bfloat16)
    query_lin = (
        jnp.dot(norm_one_low, attention_weights[0], preferred_element_type=jnp.float32) + vectors[2]
    )
    key_lin = (
        jnp.dot(norm_one_low, attention_weights[1], preferred_element_type=jnp.float32) + vectors[3]
    )
    value_low = (
        jnp.dot(norm_one_low, attention_weights[2], preferred_element_type=jnp.float32) + vectors[4]
    ).astype(jnp.bfloat16)
    rows_pos, cols_pos = patch_positions(segment, grid_height, grid_width, patch_rows, patch_cols)

    def rotary_map(flat_values, freq_values):
        return rotate_pairs(flat_values, freq_values, rows_pos, cols_pos)

    query_rot, query_back = jax.vjp(rotary_map, query_lin, freq_row)
    key_rot, key_back = jax.vjp(rotary_map, key_lin, freq_row)
    query_heads = heads_first(query_rot.astype(jnp.bfloat16))
    key_heads = heads_first(key_rot.astype(jnp.bfloat16))
    value_heads = heads_first(value_low)
    same_image = segment[:, None] == segment[None, :]
    score_scale = 1.0 / math.sqrt(model_width // HEADS)

    def head_scores(query_head, key_head):
        scores = jnp.dot(query_head, key_head.T, preferred_element_type=jnp.float32) * score_scale
        return jnp.where(same_image, scores, MASKED_SCORE)

    def head_forward(pieces):
        query_head, key_head, value_head = pieces
        scores = head_scores(query_head, key_head)
        row_peak = jnp.max(scores, axis=1, keepdims=True)
        exponent = jnp.exp(scores - row_peak)
        row_total = jnp.sum(exponent, axis=1, keepdims=True)
        weights_low = (exponent / row_total).astype(jnp.bfloat16)
        attended = jnp.dot(weights_low, value_head, preferred_element_type=jnp.float32)
        return (attended, (row_peak + jnp.log(row_total))[:, 0])

    attended_heads, log_totals = lax.map(head_forward, (query_heads, key_heads, value_heads))
    attended_low = tokens_first(attended_heads).astype(jnp.bfloat16)
    branch_one = (
        jnp.dot(attended_low, attention_weights[3], preferred_element_type=jnp.float32) + vectors[5]
    )
    middle = inputs + branch_one
    norm_two, norm_two_back = jax.vjp(layer_norm, middle, vectors[6], vectors[7])
    norm_two_low = norm_two.astype(jnp.bfloat16)
    pre_act = (
        jnp.einsum(
            "td,mde->tme", norm_two_low, up_weight, preferred_element_type=jnp.float32
        ).reshape(rows_here, -1)
        + up_bias
    )
    activation, gelu_back = jax.vjp(exact_gelu, pre_act)
    activation_blocks = activation.astype(jnp.bfloat16).reshape(rows_here, groups_mlp, -1)
    branch_two = (
        jnp.einsum(
            "tme,med->td", activation_blocks, down_weight, preferred_element_type=jnp.float32
        )
        + down_bias
    )
    grad_act = jnp.einsum(
        "td,med->tme", cotangent, down_weight, preferred_element_type=jnp.float32
    ).reshape(rows_here, -1)
    grad_down = jnp.einsum(
        "tme,td->med", activation_blocks, cotangent, preferred_element_type=jnp.float32
    )
    grad_pre_blocks = gelu_back(grad_act)[0].astype(jnp.bfloat16).reshape(rows_here, groups_mlp, -1)
    grad_up = jnp.einsum(
        "td,tme->mde", norm_two_low, grad_pre_blocks, preferred_element_type=jnp.float32
    )
    up_grad_rows = jnp.sum(grad_pre_blocks, axis=0, dtype=jnp.float32)
    grad_norm_two = jnp.einsum(
        "tme,mde->td", grad_pre_blocks, up_weight, preferred_element_type=jnp.float32
    )
    output_low = (middle + branch_two).astype(jnp.bfloat16)
    grad_middle_norm, grad_gain_two, grad_shift_two = norm_two_back(grad_norm_two)
    grad_middle = cotangent.astype(jnp.float32) + grad_middle_norm
    grad_branch_low = grad_middle.astype(jnp.bfloat16)
    grad_out_bias = jnp.sum(grad_branch_low, axis=0, dtype=jnp.float32)
    grad_out_weight = jnp.dot(attended_low.T, grad_branch_low, preferred_element_type=jnp.float32)
    grad_attended_low = jnp.dot(
        grad_branch_low, attention_weights[3].T, preferred_element_type=jnp.float32
    ).astype(jnp.bfloat16)

    def head_backward(pieces):
        query_head, key_head, value_head, grad_head, log_total = pieces
        scores = head_scores(query_head, key_head)
        probs = jnp.exp(scores - log_total[:, None])
        grad_probs = jnp.dot(grad_head, value_head.T, preferred_element_type=jnp.float32)
        inner = jnp.sum(probs * grad_probs, axis=1, keepdims=True)
        grad_scores = (probs * (grad_probs - inner)).astype(jnp.bfloat16)
        grad_query = (
            jnp.dot(grad_scores, key_head, preferred_element_type=jnp.float32) * score_scale
        )
        grad_key = (
            jnp.dot(grad_scores.T, query_head, preferred_element_type=jnp.float32) * score_scale
        )
        grad_value = jnp.dot(
            probs.astype(jnp.bfloat16).T, grad_head, preferred_element_type=jnp.float32
        )
        return (grad_query, grad_key, grad_value)

    grad_queries, grad_keys, grad_values = lax.map(
        head_backward,
        (query_heads, key_heads, value_heads, heads_first(grad_attended_low), log_totals),
    )
    grad_query_lin, grad_freq_query = query_back(tokens_first(grad_queries))
    grad_key_lin, grad_freq_key = key_back(tokens_first(grad_keys))
    grad_query_low = grad_query_lin.astype(jnp.bfloat16)
    grad_key_low = grad_key_lin.astype(jnp.bfloat16)
    grad_value_low = tokens_first(grad_values).astype(jnp.bfloat16)
    grad_query_weight = jnp.dot(norm_one_low.T, grad_query_low, preferred_element_type=jnp.float32)
    grad_key_weight = jnp.dot(norm_one_low.T, grad_key_low, preferred_element_type=jnp.float32)
    grad_value_weight = jnp.dot(norm_one_low.T, grad_value_low, preferred_element_type=jnp.float32)
    grad_norm_one = jnp.dot(
        grad_query_low, attention_weights[0].T, preferred_element_type=jnp.float32
    )
    grad_norm_one = grad_norm_one + jnp.dot(
        grad_key_low, attention_weights[1].T, preferred_element_type=jnp.float32
    )
    grad_norm_one = grad_norm_one + jnp.dot(
        grad_value_low, attention_weights[2].T, preferred_element_type=jnp.float32
    )
    grad_input_norm, grad_gain_one, grad_shift_one = norm_one_back(grad_norm_one)
    input_grad = grad_middle + grad_input_norm
    head_rows = jnp.stack(
        [
            grad_gain_one,
            grad_shift_one,
            jnp.sum(grad_query_low, axis=0, dtype=jnp.float32),
            jnp.sum(grad_key_low, axis=0, dtype=jnp.float32),
            jnp.sum(grad_value_low, axis=0, dtype=jnp.float32),
            grad_out_bias,
            grad_gain_two,
            grad_shift_two,
        ]
    )
    tail_rows = jnp.stack(
        [jnp.sum(cotangent, axis=0, dtype=jnp.float32), grad_freq_query + grad_freq_key]
    )
    local_vectors = jnp.concatenate([head_rows, up_grad_rows, tail_rows], axis=0)
    vector_sum = lax.psum(local_vectors, ("dp", "mlp"))
    attention_grads = jnp.stack(
        [grad_query_weight, grad_key_weight, grad_value_weight, grad_out_weight]
    )
    attention_share, up_share, down_share = (
        lax.psum_scatter(
            attention_grads.astype(jnp.bfloat16), "mlp", scatter_dimension=0, tiled=True
        ).astype(jnp.float32),
        lax.psum_scatter(
            grad_up.astype(jnp.bfloat16), "mlp", scatter_dimension=0, tiled=True
        ).astype(jnp.float32),
        lax.psum_scatter(
            grad_down.astype(jnp.bfloat16), "mlp", scatter_dimension=0, tiled=True
        ).astype(jnp.float32),
    )
    grad_stack = jnp.concatenate([attention_share, up_share, down_share], axis=0)
    reduced = lax.psum(grad_stack, "dp")
    block_kind = jnp.sum(jnp.where(holds_block, jnp.arange(3, dtype=jnp.int32), 0))
    owns_block = jnp.any(holds_block)
    gradient = jnp.take(reduced, block_kind, axis=0)
    decay_matrix = decays[0]
    left_old = left_slots[0, 0]
    right_old = right_slots[0, 0]
    master_old = master_slots[0, 0]
    left_next = decay_matrix * left_old + (1.0 - decay_matrix) * jnp.dot(
        gradient, gradient.T, precision=lax.Precision.HIGHEST
    )
    right_next = decay_matrix * right_old + (1.0 - decay_matrix) * jnp.dot(
        gradient.T, gradient, precision=lax.Precision.HIGHEST
    )
    direction = jnp.dot(
        jnp.dot(left_roots[0, 0], gradient, precision=lax.Precision.HIGHEST),
        right_roots[0, 0],
        precision=lax.Precision.HIGHEST,
    )
    normed_step = direction * lax.rsqrt(jnp.mean(direction * direction) + GRAFT_EPSILON)
    master_next = master_old - RATE_MATRIX * normed_step
    slot_grad = jnp.where(owns_block, gradient, 0.0)[None, None]
    left_out = jnp.where(owns_block, left_next, left_old)[None, None]
    right_out = jnp.where(owns_block, right_next, right_old)[None, None]
    master_out = jnp.where(owns_block, master_next, master_old)[None, None]
    share_width = model_width // groups_mlp

    def own_columns(table):
        return lax.dynamic_slice_in_dim(table, mlp_index * share_width, share_width, 1)

    grad_share = own_columns(vector_sum)
    moment_old = own_columns(vector_moments)
    vector_old = own_columns(vectors)
    decay_vector = decays[1]
    moment_next = decay_vector * moment_old + (1.0 - decay_vector) * grad_share * grad_share
    vector_next = vector_old - RATE_VECTOR * grad_share / (jnp.sqrt(moment_next) + STEP_EPSILON)
    return (
        output_low,
        input_grad,
        slot_grad,
        left_out,
        right_out,
        master_out,
        grad_share,
        moment_next,
        vector_next,
    )


def solution(mesh):
    placed = (
        P(("dp", "mlp"), None),
        P(("dp", "mlp"), None),
        P(),
        P(),
        P(),
        P(),
        P("dp", "mlp", None, None),
        P("dp", "mlp", None, None),
        P("dp", "mlp", None, None),
        P("dp", "mlp", None, None),
        P("dp", "mlp", None, None),
        P(("dp", "mlp")),
        P(("dp", "mlp")),
        P(("dp", "mlp")),
        P(("dp", "mlp")),
        P(("dp", "mlp")),
    )
    return jax.shard_map(
        local,
        mesh=mesh,
        in_specs=placed,
        out_specs=(
            P(("dp", "mlp"), None),
            P(("dp", "mlp"), None),
            P("dp", "mlp", None, None),
            P("dp", "mlp", None, None),
            P("dp", "mlp", None, None),
            P("dp", "mlp", None, None),
            P(None, "mlp"),
            P(None, "mlp"),
            P(None, "mlp"),
        ),
        check_vma=False,
    )
```

profile of v0, /device:TPU:0, one launch (start us, length us, event | category | flops | bytes accessed | tf_op | source)
XLA Modules:
  0.0 1202.3 jit_solution(14143546167382789815)
XLA Ops:
  14.0 278.3 %all-reduce.12 = bf16[3,768,768]{2,1,0:T(8,128)(2,1)} all-reduce(f32[3,768,768]{2,1,0:T(8,128)} %broadcast_select_fusion), channel_id=1, replica_groups=mesh['dp'=8,'mlp'=4] {'dp'}, use_global_device_ids=true, to_apply=%region_2.3 | all-reduce | flops 1769472 | bytes 10616832 | tf_op jit(solution)/shard_map/psum | solution.py:92
  303.2 78.7 %all-gather.3.cloned.1.call-done = bf16[12,768,768]{2,1,0:T(8,128)(2,1)} async-done(((bf16[3,768,768]{2,1,0:T(8,128)(2,1)}), bf16[12,768,768]{2,1,0:T(8,128)(2,1)}) %all-gather.3.cloned.1.call-update) | async-done | bytes 14155792 | tf_op jit(solution)/shard_map/all_gather | solution.py:97
  393.6 7.7 subtract_convert_fusion
  421.8 85.7 %while.32 = (s32[]{:T(128)}, bf16[12,1024,64]{1,2,0:T(8,128)(2,1)}, f32[12,1024]{1,0:T(8,128)}, bf16[12,1024,64]{2,1,0:T(8,128)(2,1)}, bf16[12,1024,64]{2,1,0:T(...) while((s32[]{:T(128)}, bf16[12,1024,64]{1,2,0:T(8,128)(2,1)}, ...), condition=%wide.region_8.9_spmd.clone.clone, body=%wide.region_5.8_spmd.clone.sunk.clone | while | flops 284163072 | bytes 13695065 | solution.py:141
  507.5 10.2 fusion.64
  517.7 12.7 %copy.133 = f32[1024,3072]{1,0:T(8,128)} copy(f32[1024,3072]{0,1:T(8,128)} %bitcast.277) | data formatting | bytes 25165824 | tf_op jit(solution)/shard_map/reshape | solution.py:165
  544.0 40.9 %convert_reduce_fusion = (f32[3072]{0:T(1024)}, bf16[1024,3072]{1,0:T(8,128)(2,1)}, f32[1024,3072]{1,0:T(8,128)}, f32[1024,3072]{1,0:T(8,128)}) fusion(f32[1024,3072]{1,0:T(8,128)S(1)} %copy-done.14, f32[3072]{0:T(1024)S(1)} %add.236, bf16[3072,768]{1,0:T(8,128)(2,1)} %bitcast.289, f32[1024,768]{0,1:T(8,128)S(1)} %get-tuple-element.370, ...), kind=kOutput, calls=%fused_computation.58 | convolution fusion | flops 5071696896 | bytes 51943424 | tf_op jit(solution)/shard_map/td,mde->tme/dot_general | solution.py:150
  584.9 12.8 %multiply_convert_fusion.1 = bf16[1024,3072]{1,0:T(8,128)(2,1)} fusion(f32[1024,3072]{1,0:T(8,128)} %get-tuple-element.336, f32[1024,3072]{1,0:T(8,128)} %get-tuple-element.371, f32[3072]{0:T(1024)S(1)} %add.236), kind=kLoop, calls=%fused_computation.60 | loop fusion | flops 12582912 | bytes 31469568 | tf_op jit(solution)/shard_map/convert_element_type | solution.py:156
  597.8 8.6 copy.137
  606.4 9.0 convolution_convert_fusion
  618.0 8.8 copy.138
  626.8 9.9 fusion.141
  655.9 10.4 convert_bitcast_fusion
  667.0 159.3 %while.33 = (s32[]{:T(128)}, f32[12,1024,64]{1,2,0:T(8,128)}, f32[12,1024,64]{1,2,0:T(8,128)}, bf16[12,1024,64]{1,2,0:T(8,128)(2,1)}, bf16[12,1024,64]{2,1,0:T(8...) while((s32[]{:T(128)}, f32[12,1024,64]{1,2,0:T(8,128)}, ...), condition=%wide.region_15.16_spmd.clone.clone, body=%wide.region_13.15_spmd.clone.sunk.clone | while | flops 681704448 | bytes 34112624 | solution.py:205
  826.3 12.0 multiply_add_fusion.1
  840.7 7.8 multiply_add_fusion
  860.6 48.4 %reduce-scatter.4.cloned.1.call-done = bf16[1,768,768]{2,1,0:T(8,128)(2,1)} async-done(((bf16[4,768,768]{2,1,0:T(8,128)(2,1)}), bf16[1,768,768]{2,1,0:T(8,128)(2,1)}) %reduce-scatter.4.cloned.1.call-update) | async-done | bytes 1179664 | tf_op jit(solution)/shard_map/reduce_scatter | solution.py:249
  919.4 10.5 fusion.75
  955.9 45.1 %psum.23 = f32[14,768]{1,0:T(8,128)S(1)} all-reduce(f32[14,768]{1,0:T(8,128)S(1)} %concatenate.21), channel_id=1, replica_groups=mesh['dp'=8,'mlp'=4] {'dp','mlp'}, use_global_device_ids=true, to_apply=%region_39.40 | all-reduce | flops 10752 | bytes 86016 | tf_op jit(solution)/shard_map/psum | solution.py:244
  1003.1 143.9 %all-reduce.11.cloned.1.call-done = f32[3,768,768]{2,1,0:T(8,128)} async-done(((f32[3,768,768]{2,1,0:T(8,128)}), f32[3,768,768]{2,1,0:T(8,128)}) %all-reduce.11.cloned.1.call-update) | async-done | bytes 7077904 | tf_op jit(solution)/shard_map/psum | solution.py:260
  1147.1 13.6 %fusion.79 = f32[768,768]{1,0:T(8,128)S(1)} fusion(f32[1,1,768,768]{3,2,1,0:T(8,128)} %param.29, f32[3,768,768]{2,1,0:T(8,128)} %all-reduce.11.cloned.1.call-done, s32[]{:T(128)S(6)} %select_n.95, pred[]{:T(512)S(6)} %and.13), kind=kOutput, calls=%fused_computation.124 | convolution fusion | flops 5436407808 | bytes 7077893 | tf_op jit(solution)/shard_map/dot_general | solution.py:275
  1160.7 8.7 multiply_reduce_fusion.4
  1177.5 8.9 fusion.84
  1186.4 9.2 fusion.82
  (355 shorter events, 387.2 us)
Async XLA Ops:
  7.2 1153.5 %copy-start = (f32[1,1,768,768]{3,2,1,0:T(8,128)S(1)}, f32[1,1,768,768]{3,2,1,0:T(8,128)}, u32[]{:S(2)}) copy-start(f32[1,1,768,768]{3,2,1,0:T(8,128)} %param.30) | copy-start | bytes 7077892
  7.2 374.6 %all-gather.3.cloned.1.call-start = ((), (), s32[]{:S(2)}) async-start(), calls=%async_computation.7 | async-start | bytes 17694720 | tf_op jit(solution)/shard_map/all_gather | solution.py:97
  292.3 568.3 %reduce-scatter.8.cloned.1.call-start = ((), (), s32[]{:S(2)}) async-start(), calls=%async_computation.5 | async-start | bytes 5898240 | tf_op jit(solution)/shard_map/reduce_scatter | solution.py:255
  294.8 8.3 copy-start.51
  297.5 96.0 %copy-start.28 = (f32[12,32]{1,0:T(8,128)}, f32[12,32]{1,0:T(8,128)S(1)}, u32[]{:S(2)}) copy-start(f32[12,32]{1,0:T(8,128)S(1)} %mul.390) | copy-start | bytes 4612
  297.6 95.9 %copy-start.30 = (f32[12,32]{1,0:T(8,128)}, f32[12,32]{1,0:T(8,128)S(1)}, u32[]{:S(2)}) copy-start(f32[12,32]{1,0:T(8,128)S(1)} %mul.385) | copy-start | bytes 4612
  298.4 114.8 %copy-start.40 = (f32[768]{0:T(1024)}, f32[768]{0:T(1024)S(1)}, u32[]{:S(2)}) copy-start(f32[768]{0:T(1024)S(1)} %get-tuple-element.290) | copy-start | bytes 9220
  298.4 114.8 %copy-start.48 = (f32[768]{0:T(1024)}, f32[768]{0:T(1024)S(1)}, u32[]{:S(2)}) copy-start(f32[768]{0:T(1024)S(1)} %get-tuple-element.289) | copy-start | bytes 9220
  300.4 112.8 %copy-start.32 = (f32[1024]{0:T(1024)}, f32[1024]{0:T(1024)S(1)}, u32[]{:S(2)}) copy-start(f32[1024]{0:T(1024)S(1)} %broadcast_multiply_fusion.1) | copy-start | bytes 12292
  302.5 110.7 %copy-start.42 = (f32[1024]{0:T(1024)}, f32[1024]{0:T(1024)S(1)}, u32[]{:S(2)}) copy-start(f32[1024]{0:T(1024)S(1)} %fusion.118) | copy-start | bytes 12292
  303.1 90.4 %copy-start.34 = (f32[1024]{0:T(1024)}, f32[1024]{0:T(1024)S(1)}, u32[]{:S(2)}) copy-start(f32[1024]{0:T(1024)S(1)} %get-tuple-element.377) | copy-start | bytes 12292
  303.1 90.4 %copy-start.36 = (f32[1024]{0:T(1024)}, f32[1024]{0:T(1024)S(1)}, u32[]{:S(2)}) copy-start(f32[1024]{0:T(1024)S(1)} %get-tuple-element.378) | copy-start | bytes 12292
  541.0 43.9 %copy-start.4 = (f32[1024,768]{0,1:T(8,128)}, f32[1024,768]{0,1:T(8,128)S(1)}, u32[]{:S(2)}) copy-start(f32[1024,768]{0,1:T(8,128)S(1)} %get-tuple-element.370) | copy-start | bytes 9437188
  615.4 245.2 %reduce-scatter.6.cloned.1.call-start = ((), (), s32[]{:S(2)}) async-start(), calls=%async_computation.4 | async-start | bytes 5898240 | tf_op jit(solution)/shard_map/reduce_scatter | solution.py:252
  666.3 242.7 %reduce-scatter.4.cloned.1.call-start = ((), (), s32[]{:S(2)}) async-start(), calls=%async_computation.3 | async-start | bytes 5898240 | tf_op jit(solution)/shard_map/reduce_scatter | solution.py:249
  667.0 159.3 %copy-start.29 = (f32[12,32]{1,0:T(8,128)S(1)}, f32[12,32]{1,0:T(8,128)}, u32[]{:S(2)}) copy-start(f32[12,32]{1,0:T(8,128)} %copy-done.28) | copy-start | bytes 4612
  667.0 159.3 %copy-start.31 = (f32[12,32]{1,0:T(8,128)S(1)}, f32[12,32]{1,0:T(8,128)}, u32[]{:S(2)}) copy-start(f32[12,32]{1,0:T(8,128)} %copy-done.30) | copy-start | bytes 4612
  667.0 159.3 %copy-start.35 = (f32[1024]{0:T(1024)S(1)}, f32[1024]{0:T(1024)}, u32[]{:S(2)}) copy-start(f32[1024]{0:T(1024)} %copy-done.34) | copy-start | bytes 12292
  667.0 159.3 %copy-start.37 = (f32[1024]{0:T(1024)S(1)}, f32[1024]{0:T(1024)}, u32[]{:S(2)}) copy-start(f32[1024]{0:T(1024)} %copy-done.36) | copy-start | bytes 12292
  826.3 12.3 %copy-start.18 = (f32[12,1024,64]{1,2,0:T(8,128)S(1)}, f32[12,1024,64]{1,2,0:T(8,128)}, u32[]{:S(2)}) copy-start(f32[12,1024,64]{1,2,0:T(8,128)} %get-tuple-element.104) | copy-start | bytes 9437188
  838.5 17.7 %copy-start.25 = (bf16[1024,12,64]{0,2,1:T(8,128)(2,1)}, bf16[1024,12,64]{0,2,1:T(8,128)(2,1)S(1)}, u32[]{:S(2)}) copy-start(bf16[1024,12,64]{0,2,1:T(8,128)(2,1)S(1)} %get-tuple-element.342) | copy-start | bytes 4718596
  860.3 286.7 %all-reduce.11.cloned.1.call-start = ((), (), s32[]{:S(2)}) async-start(), calls=%async_computation.6 | async-start | bytes 14155776 | tf_op jit(solution)/shard_map/psum | solution.py:260
  951.0 50.0 %copy-start.39 = (f32[14,768]{1,0:T(8,128)S(1)}, f32[14,768]{1,0:T(8,128)}, u32[]{:S(2)}) copy-start(f32[14,768]{1,0:T(8,128)} %param.22) | copy-start | bytes 129028
  1177.5 8.9 copy-start.56
  (39 other events, 130.4 us)
Sparse Core Ops, SparseCore 0:
  292.4 89.3 all-gather.2
  615.5 47.9 reduce-scatter.7
  666.4 48.3 reduce-scatter.5
  860.4 48.5 reduce-scatter.3
  914.5 232.5 all-reduce.10
where the time goes:
time: 1220 us; the launch traced here: 1200 us
  matrix products  359 us (29%)
  blocking collectives  323 us (26%)
  waiting for transfers between devices  271 us (22%)
  local copies, waits for them, and re-layouts  115 us (9%)
  other arithmetic  115 us (9%)
  between operations  18.4 us (2%)
    psum x1, blocking collectives, local(): blocks = lax.psum(owned_blocks, 'dp')  278 us
    psum x1, waiting for transfers between devices, local(): reduced = lax.psum(grad_stack, 'dp')  144 us
    all_gather x1, waiting for transfers between devices, local(): every_block = lax.all_gather(blocks_low[None], 'mlp', axis=0, tiled=True)  78.7 us
    dot_general x24, matrix products, head_scores(): jnp.dot(query_head, key_head.T, preferred_element_type=jnp.float32)  52.2 us
    reduce_scatter x1, waiting for transfers between devices, local(): lax.psum_scatter(attention_grads.astype(jnp.bfloat16), 'mlp', scatter_dim...  48.4 us
    psum x1, blocking collectives, local(): vector_sum = lax.psum(local_vectors, ('dp', 'mlp'))  45.1 us
    dot_general x1, matrix products, local(): jnp.einsum('td,mde->tme', norm_two_low, up_weight, preferred_element_type...  40.9 us
    dot_general x12, matrix products, head_forward(): jnp.dot(weights_low, value_head, preferred_element_type=jnp.float32)  35.5 us
  transfers between devices with their start and end apart: 5, of which 3 were waited for; matrix products, arithmetic and copies ran while one was open for 24% of the time, Pallas kernels for 0%

commit v1 on v0

--- a/solution.py
+++ b/solution.py
@@ -257,7 +257,7 @@
         ).astype(jnp.float32),
     )
     grad_stack = jnp.concatenate([attention_share, up_share, down_share], axis=0)
-    reduced = lax.psum(grad_stack, "dp")
+    reduced = jnp.sum(lax.all_gather(grad_stack, "dp"), axis=0)
     block_kind = jnp.sum(jnp.where(holds_block, jnp.arange(3, dtype=jnp.int32), 0))
     owns_block = jnp.any(holds_block)
     gradient = jnp.take(reduced, block_kind, axis=0)

time: 1220 us -> 2090 us (1.71)
  waiting for transfers between devices: 271 us -> 1060 us
  blocking collectives: 323 us -> 370 us
  other arithmetic: 115 us -> 138 us
    all_gather x0 -> x1, waiting for transfers between devices: none -> 937 us  [local(): reduced = jnp.sum(lax.all_gather(grad_stack, 'dp'), axis=0)]
    psum x1 -> x0, waiting for transfers between devices: 144 us -> none  [local(): reduced = lax.psum(grad_stack, 'dp')]
    psum x1, blocking collectives: 45.1 us -> 91.3 us  [local(): vector_sum = lax.psum(local_vectors, ('dp', 'mlp'))]
    reduce_sum x0 -> x1, other arithmetic: none -> 21.5 us  [local(): reduced = jnp.sum(lax.all_gather(grad_stack, 'dp'), axis=0)]
  transfers between devices with their start and end apart: 5 -> 5, of which waited for: 3 -> 3; matrix products, arithmetic and copies ran while one was open for 24% -> 14% of each run, Pallas kernels for 0% -> 0%
where the time goes in v1:
time: 2090 us; the launch traced here: 2080 us
  waiting for transfers between devices  1060 us (51%)
  matrix products  371 us (18%)
  blocking collectives  370 us (18%)
  other arithmetic  138 us (7%)
  local copies, waits for them, and re-layouts  115 us (6%)
    all_gather x1, waiting for transfers between devices, local(): reduced = jnp.sum(lax.all_gather(grad_stack, 'dp'), axis=0)  937 us
    psum x1, blocking collectives, local(): blocks = lax.psum(owned_blocks, 'dp')  278 us
    psum x1, blocking collectives, local(): vector_sum = lax.psum(local_vectors, ('dp', 'mlp'))  91.3 us
    all_gather x1, waiting for transfers between devices, local(): every_block = lax.all_gather(blocks_low[None], 'mlp', axis=0, tiled=True)  78.6 us
    dot_general x24, matrix products, head_scores(): jnp.dot(query_head, key_head.T, preferred_element_type=jnp.float32)  52.2 us
    reduce_scatter x1, waiting for transfers between devices, local(): lax.psum_scatter(attention_grads.astype(jnp.bfloat16), 'mlp', scatter_dim...  48.2 us
  transfers between devices with their start and end apart: 5, of which 3 were waited for; matrix products, arithmetic and copies ran while one was open for 14% of the time, Pallas kernels for 0%

profile of v1, /device:TPU:0, one launch (start us, length us, event | category | flops | bytes accessed | tf_op | source)
XLA Modules:
  0.0 2076.7 jit_solution(3306265024773778636)
XLA Ops:
  14.0 278.3 %all-reduce.9 = bf16[3,768,768]{2,1,0:T(8,128)(2,1)} all-reduce(f32[3,768,768]{2,1,0:T(8,128)} %broadcast_select_fusion), channel_id=1, replica_groups=mesh['dp'=8,'mlp'=4] {'dp'}, use_global_device_ids=true, to_apply=%region_2.3 | all-reduce | flops 1769472 | bytes 10616832 | tf_op jit(solution)/shard_map/psum | solution.py:92
  303.2 78.6 %all-gather.5.cloned.1.call-done = bf16[12,768,768]{2,1,0:T(8,128)(2,1)} async-done(((bf16[3,768,768]{2,1,0:T(8,128)(2,1)}), bf16[12,768,768]{2,1,0:T(8,128)(2,1)}) %all-gather.5.cloned.1.call-update) | async-done | bytes 14155792 | tf_op jit(solution)/shard_map/all_gather | solution.py:97
  421.8 85.7 %while.32 = (s32[]{:T(128)}, bf16[12,1024,64]{1,2,0:T(8,128)(2,1)}, f32[12,1024]{1,0:T(8,128)}, bf16[12,1024,64]{2,1,0:T(8,128)(2,1)}, bf16[12,1024,64]{2,1,0:T(...) while((s32[]{:T(128)}, bf16[12,1024,64]{1,2,0:T(8,128)(2,1)}, ...), condition=%wide.region_8.9_spmd.clone.clone, body=%wide.region_5.8_spmd.clone.sunk.clone | while | flops 284163072 | bytes 13695065 | solution.py:141
  507.5 21.6 %fusion.64 = f32[4,768,1024]{2,1,0:T(8,128)} fusion(bf16[4,3,768,768]{3,2,1,0:T(8,128)(2,1)} %bitcast.298, bf16[1024,768]{1,0:T(8,128)(2,1)} %param.21), kind=kOutput, calls=%fused_computation.88 | convolution fusion | flops 4831838208 | bytes 18874368 | tf_op jit(solution)/shard_map/td,med->tme/dot_general | solution.py:163
  529.2 12.6 copy.133
  555.4 41.0 %convert_reduce_fusion = (f32[3072]{0:T(1024)}, bf16[1024,3072]{1,0:T(8,128)(2,1)}, f32[1024,3072]{1,0:T(8,128)}, f32[1024,3072]{1,0:T(8,128)}) fusion(f32[1024,3072]{1,0:T(8,128)S(1)} %copy-done.15, f32[3072]{0:T(1024)S(1)} %add.234, bf16[3072,768]{1,0:T(8,128)(2,1)} %bitcast.291, f32[1024,768]{0,1:T(8,128)S(1)} %get-tuple-element.370, ...), kind=kOutput, calls=%fused_computation.58 | convolution fusion | flops 5071696896 | bytes 51943424 | tf_op jit(solution)/shard_map/td,mde->tme/dot_general | solution.py:150
  596.4 12.8 multiply_convert_fusion.1
  609.2 8.7 copy.137
  617.9 9.0 convolution_convert_fusion
  629.6 8.8 copy.138
  638.4 9.8 fusion.141
  667.5 10.4 convert_bitcast_fusion
  678.5 159.2 %while.33 = (s32[]{:T(128)}, f32[12,1024,64]{1,2,0:T(8,128)}, f32[12,1024,64]{1,2,0:T(8,128)}, bf16[12,1024,64]{1,2,0:T(8,128)(2,1)}, bf16[12,1024,64]{2,1,0:T(8...) while((s32[]{:T(128)}, f32[12,1024,64]{1,2,0:T(8,128)}, ...), condition=%wide.region_15.16_spmd.clone.clone, body=%wide.region_13.15_spmd.clone.sunk.clone | while | flops 681704448 | bytes 34112624 | solution.py:205
  837.8 12.0 multiply_add_fusion.1
  852.2 7.8 multiply_add_fusion
  872.3 48.2 %reduce-scatter.4.cloned.1.call-done = bf16[1,768,768]{2,1,0:T(8,128)(2,1)} async-done(((bf16[4,768,768]{2,1,0:T(8,128)(2,1)}), bf16[1,768,768]{2,1,0:T(8,128)(2,1)}) %reduce-scatter.4.cloned.1.call-update) | async-done | bytes 1179664 | tf_op jit(solution)/shard_map/reduce_scatter | solution.py:249
  931.0 10.8 fusion.75
  967.7 91.3 %psum.15 = f32[14,768]{1,0:T(8,128)S(1)} all-reduce(f32[14,768]{1,0:T(8,128)S(1)} %concatenate.18), channel_id=1, replica_groups=mesh['dp'=8,'mlp'=4] {'dp','mlp'}, use_global_device_ids=true, to_apply=%region_39.40 | all-reduce | flops 10752 | bytes 86016 | tf_op jit(solution)/shard_map/psum | solution.py:244
  1061.1 936.6 %all-gather.7.cloned.1.call-done = f32[24,768,768]{2,1,0:T(8,128)} async-done(((f32[3,768,768]{2,1,0:T(8,128)}), f32[24,768,768]{2,1,0:T(8,128)}) %all-gather.7.cloned.1.call-update) | async-done | bytes 56623120 | tf_op jit(solution)/shard_map/all_gather | solution.py:260
  1997.7 21.5 %reduce_sum.277 = f32[3,768,768]{2,1,0:T(8,128)} reduce(f32[8,3,768,768]{3,2,1,0:T(8,128)} %bitcast.276, f32[]{:T(128)} %constant.45.clone.1), dimensions={0}, to_apply=%region_23.24 | reduce | flops 12386304 | bytes 63700996 | tf_op jit(solution)/shard_map/reduce_sum | solution.py:260
  2023.7 11.4 fusion.84
  2035.1 9.1 fusion.82
  2044.2 11.5 fusion.79
  2055.7 8.6 multiply_reduce_fusion.4
  (358 shorter events, 397.0 us)
Async XLA Ops:
  7.2 2048.5 %copy-start = (f32[1,1,768,768]{3,2,1,0:T(8,128)S(1)}, f32[1,1,768,768]{3,2,1,0:T(8,128)}, u32[]{:S(2)}) copy-start(f32[1,1,768,768]{3,2,1,0:T(8,128)} %param.30) | copy-start | bytes 7077892
  7.2 374.6 %all-gather.5.cloned.1.call-start = ((), (), s32[]{:S(2)}) async-start(), calls=%async_computation.6 | async-start | bytes 17694720 | tf_op jit(solution)/shard_map/all_gather | solution.py:97
  292.3 580.0 %reduce-scatter.8.cloned.1.call-start = ((), (), s32[]{:S(2)}) async-start(), calls=%async_computation.5 | async-start | bytes 5898240 | tf_op jit(solution)/shard_map/reduce_scatter | solution.py:255
  297.5 95.9 %copy-start.29 = (f32[12,32]{1,0:T(8,128)}, f32[12,32]{1,0:T(8,128)S(1)}, u32[]{:S(2)}) copy-start(f32[12,32]{1,0:T(8,128)S(1)} %mul.390) | copy-start | bytes 4612
  297.6 95.9 %copy-start.31 = (f32[12,32]{1,0:T(8,128)}, f32[12,32]{1,0:T(8,128)S(1)}, u32[]{:S(2)}) copy-start(f32[12,32]{1,0:T(8,128)S(1)} %mul.385) | copy-start | bytes 4612
  298.4 114.8 %copy-start.41 = (f32[768]{0:T(1024)}, f32[768]{0:T(1024)S(1)}, u32[]{:S(2)}) copy-start(f32[768]{0:T(1024)S(1)} %get-tuple-element.290) | copy-start | bytes 9220
  298.4 114.8 %copy-start.49 = (f32[768]{0:T(1024)}, f32[768]{0:T(1024)S(1)}, u32[]{:S(2)}) copy-start(f32[768]{0:T(1024)S(1)} %get-tuple-element.289) | copy-start | bytes 9220
  300.4 112.9 %copy-start.33 = (f32[1024]{0:T(1024)}, f32[1024]{0:T(1024)S(1)}, u32[]{:S(2)}) copy-start(f32[1024]{0:T(1024)S(1)} %broadcast_multiply_fusion.1) | copy-start | bytes 12292
  302.6 110.7 %copy-start.43 = (f32[1024]{0:T(1024)}, f32[1024]{0:T(1024)S(1)}, u32[]{:S(2)}) copy-start(f32[1024]{0:T(1024)S(1)} %fusion.118) | copy-start | bytes 12292
  303.2 90.4 %copy-start.35 = (f32[1024]{0:T(1024)}, f32[1024]{0:T(1024)S(1)}, u32[]{:S(2)}) copy-start(f32[1024]{0:T(1024)S(1)} %get-tuple-element.377) | copy-start | bytes 12292
  303.2 90.4 %copy-start.37 = (f32[1024]{0:T(1024)}, f32[1024]{0:T(1024)S(1)}, u32[]{:S(2)}) copy-start(f32[1024]{0:T(1024)S(1)} %get-tuple-element.378) | copy-start | bytes 12292
  552.4 44.0 %copy-start.4 = (f32[1024,768]{0,1:T(8,128)}, f32[1024,768]{0,1:T(8,128)S(1)}, u32[]{:S(2)}) copy-start(f32[1024,768]{0,1:T(8,128)S(1)} %get-tuple-element.370) | copy-start | bytes 9437188
  626.9 245.4 %reduce-scatter.6.cloned.1.call-start = ((), (), s32[]{:S(2)}) async-start(), calls=%async_computation.4 | async-start | bytes 5898240 | tf_op jit(solution)/shard_map/reduce_scatter | solution.py:252
  677.9 242.6 %reduce-scatter.4.cloned.1.call-start = ((), (), s32[]{:S(2)}) async-start(), calls=%async_computation.3 | async-start | bytes 5898240 | tf_op jit(solution)/shard_map/reduce_scatter | solution.py:249
  678.5 159.2 %copy-start.30 = (f32[12,32]{1,0:T(8,128)S(1)}, f32[12,32]{1,0:T(8,128)}, u32[]{:S(2)}) copy-start(f32[12,32]{1,0:T(8,128)} %copy-done.29) | copy-start | bytes 4612
  678.5 159.2 %copy-start.32 = (f32[12,32]{1,0:T(8,128)S(1)}, f32[12,32]{1,0:T(8,128)}, u32[]{:S(2)}) copy-start(f32[12,32]{1,0:T(8,128)} %copy-done.31) | copy-start | bytes 4612
  678.5 159.2 %copy-start.36 = (f32[1024]{0:T(1024)S(1)}, f32[1024]{0:T(1024)}, u32[]{:S(2)}) copy-start(f32[1024]{0:T(1024)} %copy-done.35) | copy-start | bytes 12292
  678.5 159.2 %copy-start.38 = (f32[1024]{0:T(1024)S(1)}, f32[1024]{0:T(1024)}, u32[]{:S(2)}) copy-start(f32[1024]{0:T(1024)} %copy-done.37) | copy-start | bytes 12292
  837.8 12.2 copy-start.19
  850.0 17.7 copy-start.26
  871.8 1125.9 %all-gather.7.cloned.1.call-start = ((), (), s32[]{:S(2)}) async-start(), calls=%async_computation.7 | async-start | bytes 63700992 | tf_op jit(solution)/shard_map/all_gather | solution.py:260
  962.9 96.2 %copy-start.40 = (f32[14,768]{1,0:T(8,128)S(1)}, f32[14,768]{1,0:T(8,128)}, u32[]{:S(2)}) copy-start(f32[14,768]{1,0:T(8,128)} %param.22) | copy-start | bytes 129028
  2019.2 15.9 copy-start.57
  2023.7 11.4 copy-start.12
  (40 other events, 145.0 us)
Sparse Core Ops, SparseCore 0:
  292.4 89.3 all-gather.4
  627.0 47.9 reduce-scatter.7
  678.0 48.3 reduce-scatter.5
  871.9 48.5 reduce-scatter.3
  926.0 1071.6 all-gather.6
